TPU v7x, 128 devices: a whole 4x4x4 slice. The times are simulated.
128 devices in a mesh: rows: 128 (over x, y, z, core).
Axes of the slice: x: 4, y: 4, z: 4, core: 2. Of those that a mesh axis runs over, the one named last changes fastest.
Arguments:
- right_side: float32 [9, 16384], P(None, 'rows'), may hold values from -30 to 30
- diag_blocks: float32 [9, 9, 16384], P(None, None, 'rows'), may hold values from -40 to 45, as said below
- precond: float32 [9, 9, 16384], P(None, None, 'rows'), may hold values from -5 to 5, as said below
- upper_blocks: float32 [8, 9, 9, 16384], P(None, None, None, 'rows'), may hold values from -0.21875 to 0.21875
- block_cols: int32 [8, 16384], P(None, 'rows'), may hold values from 0 to 16383, as said below
- slot_of_camera: int32 [16384], replicated, may hold values from 0 to 16383, as said below
Outputs:
- solution: float32 [9, 16384], P(None, 'rows')
- residual: float32 [9, 16384], P(None, 'rows')
Inputs may be any that keep to these rules, and one draw needn't show every extreme that they name: slot_of_camera is a permutation; slot s is held by the device s // 128. `block_cols`: for every device d and every device e, exactly 8 of the entries of the lists of the rows held by d name cameras whose slot is held by e. A list may name a camera more than once, or the row's own camera; every entry adds its block. `diag_blocks`: each 9 x 9 block over the first two dimensions is symmetric positive definite. `precond`: each 9 x 9 block over the first two dimensions is symmetric positive definite.
All inputs are finite; a program needn't handle non-finite values.
Results may differ from a plain program's by a relative error of at most 0.0001.
Values sent between devices are 32-bit elements; how exact they have to be, the bound alone decides.
A program may use at most 64 MiB of HBM per device.

v0:
```python
import jax
import jax.numpy as jnp
from jax import lax
from jax.sharding import Mesh
from jax.sharding import PartitionSpec as P

BLOCK = 9
ITERS = 2
ROWS = ("rows_0", "rows_1", "rows_2", "rows_3")


def side_by_side(arrays, axis, split_dim, concat_dim, along):
    ends, at = ([], 0)
    for a in arrays[:-1]:
        at += a.shape[along]
        ends.append(at)
    both = jnp.concatenate(arrays, axis=along)
    return tuple(
        jnp.split(
            lax.all_to_all(both, axis, split_axis=split_dim, concat_axis=concat_dim, tiled=True),
            ends,
            axis=along,
        )
    )


def one_axis_at_a_time(x, axes):
    for axis in axes:
        x = lax.psum(x, axis)
    return x


def local(right_side, diag_blocks, precond, upper_blocks, block_cols, slot_of_camera):
    highest = lax.Precision.HIGHEST
    cam_rows = right_side.shape[1]
    list_len = block_cols.shape[0]
    devices = lax.axis_size(ROWS)
    slot_lists = slot_of_camera[block_cols]
    flat_slots = slot_lists.reshape(-1)
    owners = flat_slots // cam_rows
    offsets = flat_slots % cam_rows
    bucket_order = jnp.argsort(owners, stable=True)
    inverse_order = jnp.argsort(bucket_order)
    wanted = offsets[bucket_order].reshape(devices, -1)
    requested = lax.all_to_all(wanted, ROWS, split_axis=0, concat_axis=0, tiled=True)
    requested_flat = requested.reshape(-1)
    solution = jnp.zeros_like(right_side)
    residual = right_side
    direction = jnp.zeros_like(right_side)
    along = jnp.zeros_like(right_side)
    old_dot = jnp.float32(1.0)
    step_size = jnp.float32(1.0)
    for step in range(ITERS):
        precond_res = jnp.einsum("abc,bc->ac", precond, residual, precision=highest)
        result = jnp.einsum("abc,bc->ac", diag_blocks, precond_res, precision=highest)
        spread = jnp.einsum("kabc,ac->bkc", upper_blocks, precond_res, precision=highest).reshape(
            BLOCK, -1
        )
        answers = precond_res[:, requested_flat].reshape(BLOCK, devices, -1)
        outgoing = spread[:, bucket_order].reshape(BLOCK, devices, -1)
        fetched, pushed = side_by_side((answers, outgoing), ROWS, 1, 1, 0)
        gathered = fetched.reshape(BLOCK, -1)[:, inverse_order].reshape(BLOCK, list_len, cam_rows)
        result = result + jnp.einsum("kabc,bkc->ac", upper_blocks, gathered, precision=highest)
        result = result.at[:, requested_flat].add(pushed.reshape(BLOCK, -1))
        res_dot, curve_dot = (
            one_axis_at_a_time(jnp.sum(residual * precond_res), ROWS),
            one_axis_at_a_time(jnp.sum(result * precond_res), ROWS),
        )
        if step == 0:
            step_size = res_dot / curve_dot
            direction = precond_res
            along = result
        else:
            momentum = res_dot / old_dot
            step_size = res_dot / (curve_dot - momentum * res_dot / step_size)
            direction = precond_res + momentum * direction
            along = result + momentum * along
        solution = solution + step_size * direction
        residual = residual - step_size * along
        old_dot = res_dot
    return (solution, residual)


def solution(mesh):
    finer = Mesh(mesh.devices.reshape(4, 4, 4, 2), ("rows_0", "rows_1", "rows_2", "rows_3"))
    return jax.shard_map(
        local,
        mesh=finer,
        in_specs=(
            P(None, ROWS),
            P(None, None, ROWS),
            P(None, None, ROWS),
            P(None, None, None, ROWS),
            P(None, ROWS),
            P(),
        ),
        out_specs=(P(None, ROWS), P(None, ROWS)),
        check_vma=False,
    )
```

profile of v0, /device:TPU:1, one launch (start us, length us, event | category | flops | bytes accessed | tf_op | source)
XLA Modules:
  0.0 224.4 jit_solution(4263776714419083464)
XLA Ops:
  0.7 0.7 fusion.11
  1.5 6.1 %gather_fusion = s32[1024]{0:T(1024)S(1)} fusion(s32[16384]{0:T(1024)S(1)} %copy-done, s32[1024]{0:T(1024)S(1)} %fusion.11), kind=kCustom, calls=%fused_computation | custom fusion | bytes 12288 | tf_op jit(solution)/shard_map/gather | solution.py:38
  7.7 4.4 %sort.34 = (s32[1024]{0:T(1024)}, s32[1024]{0:T(1024)S(1)}) sort(s32[1024]{0:T(1024)S(1)} %get-tuple-element.39, s32[1024]{0:T(1024)S(1)} %iota.8), dimensions={0}, to_apply=%region_5.6 | sort | flops 10240 | bytes 16384 | tf_op jit(solution)/shard_map/jit(argsort)/sort | solution.py:42
  12.0 4.5 %gather_fusion.1 = s32[1024]{0:T(1024)S(1)} fusion(s32[1024]{0:T(1024)S(1)} %get-tuple-element.38, s32[1024]{0:T(1024)S(1)} %fusion.12), kind=kCustom, calls=%fused_computation.1 | custom fusion | bytes 12288 | tf_op jit(solution)/shard_map/gather | solution.py:44
  16.6 0.7 all_to_all.12
  17.3 11.5 %all-to-all-start = ((s32[128,1,8]{2,1,0:T(1,128)}), s32[128,1,8]{2,1,0:T(1,128)S(1)}, u32[]{:S(2)}, u32[]{:S(2)}) async-start(s32[128,1,8]{2,1,0:T(1,128)} %bitcast.8), calls=%async_computation | async-start | bytes 131072 | tf_op jit(solution)/shard_map/all_to_all | solution.py:45
  28.9 8.2 %copy.71 = f32[8,9,9,128]{2,1,0,3:T(8,128)} copy(f32[8,9,9,128]{3,0,2,1:T(8,128)S(1)} %copy-done.1) | data formatting | bytes 663552 | tf_op args[3]
  37.1 0.5 copy.68
  37.7 6.5 %fusion.19 = f32[128,1,8,9]{3,1,2,0:T(1,128)S(1)} fusion(f32[9,128,1,1]{0,2,3,1:T(1,128)S(1)} %bitcast.116, f32[8,9,9,128]{2,1,0,3:T(8,128)} %copy.71), kind=kOutput, calls=%fused_computation.56 | convolution fusion | flops 995328 | bytes 373248 | tf_op jit(solution)/shard_map/kabc,ac->bkc/dot_general | solution.py:56
  44.2 1.0 fusion.18
  45.3 2.8 %gather_fusion.3 = f32[1024,9]{1,0:T(8,128)S(1)} fusion(f32[9,1024]{0,1:T(8,128)S(1)} %bitcast.127, s32[1024]{0:T(1024)S(1)} %fusion.12), kind=kCustom, calls=%fused_computation.3 | custom fusion | bytes 77824 | tf_op jit(solution)/shard_map/gather | solution.py:60
  48.1 4.4 %sort.35 = (s32[1024]{0:T(1024)}, s32[1024]{0:T(1024)S(1)}) sort(s32[1024]{0:T(1024)S(1)} %get-tuple-element.4, s32[1024]{0:T(1024)S(1)} %iota.9), dimensions={0}, to_apply=%region_6.7 | sort | flops 10240 | bytes 16384 | tf_op jit(solution)/shard_map/jit(argsort)/sort | solution.py:43
  52.5 0.5 broadcast.66
  53.0 0.8 reduce.5
  53.9 2.8 %gather_fusion.2 = f32[1024,9]{1,0:T(8,128)S(1)} fusion(f32[9,128]{0,1:T(8,128)S(1)} %bitcast.118, s32[1024]{0:T(1024)S(1)} %broadcast_clamp_fusion), kind=kCustom, calls=%fused_computation.2 | custom fusion | bytes 77824 | tf_op jit(solution)/shard_map/gather | solution.py:59
  57.0 1.0 reshape.210
  58.0 9.8 %all-to-all-start.1 = ((f32[128,1,144]{2,1,0:T(1,128)}), f32[128,1,144]{2,1,0:T(1,128)S(1)}, u32[]{:S(2)}, u32[]{:S(2)}) async-start(f32[128,1,144]{2,1,0:T(1,128)} %reshape.210), calls=%async_computation.1 | async-start | bytes 262144 | tf_op jit(solution)/shard_map/all_to_all | solution.py:20
  67.8 8.1 %copy.74 = f32[8,9,9,128]{1,2,0,3:T(8,128)} copy(f32[8,9,9,128]{3,0,2,1:T(8,128)S(1)} %copy-done.1) | data formatting | bytes 663552 | tf_op args[3]
  76.0 0.5 copy.77
  76.6 1.0 all-to-all-done.1
  78.0 1.0 reduce.6
  79.3 4.0 %gather_fusion.4 = f32[1024,9]{1,0:T(8,128)} fusion(f32[9,1024]{0,1:T(8,128)S(1)} %slice_bitcast_fusion.5, s32[1024]{0:T(1024)S(1)} %fusion.13), kind=kCustom, calls=%fused_computation.4 | custom fusion | bytes 77824 | tf_op jit(solution)/shard_map/gather | solution.py:62
  83.3 9.7 %fusion.4 = f32[128,1,9,1]{2,1,3,0:T(1,128)S(1)} fusion(f32[8,9,9,128]{1,2,0,3:T(8,128)} %copy.74, f32[9,8,128,1]{0,2,1,3:T(8,128)} %bitcast.134), kind=kOutput, calls=%fused_computation.20 | convolution fusion | flops 995328 | bytes 373248 | tf_op jit(solution)/shard_map/kabc,bkc->ac/dot_general | solution.py:63
  93.0 6.3 %scatter_custom_fusion = f32[9,128]{0,1:T(8,128)S(1)} fusion(f32[9,128]{0,1:T(8,128)S(1)} %add_bitcast_fusion.1, s32[1024]{0:T(1024)S(1)} %bitcast.141, f32[18,128,8]{0,2,1:T(8,128)S(1)} %bitcast.125), kind=kCustom, calls=%fused_computation.14 | custom fusion | flops 9216 | bytes 528896 | tf_op jit(solution)/shard_map/scatter-add | solution.py:64
  99.4 0.7 multiply_reduce_fusion.3
  100.1 8.2 %all-reduce.5 = (f32[]{:T(128)}, f32[]{:T(128)}) all-reduce(f32[]{:T(128)} %get-tuple-element.21, f32[]{:T(128)} %get-tuple-element.20), channel_id=1, replica_groups=mesh['rows_0'=4,'rows_1'=4,'rows_2'=4,'rows_3'=2] {'rows_0'}, use_global_device_ids=true, to_apply=%region_1.2 | all-reduce | flops 2 | bytes 16 | tf_op jit(solution)/shard_map/psum | solution.py:29
  108.3 9.2 %all-reduce.3 = (f32[]{:T(128)}, f32[]{:T(128)}) all-reduce(f32[]{:T(128)} %get-tuple-element.32, f32[]{:T(128)} %get-tuple-element.33), channel_id=1, replica_groups=mesh['rows_0'=4,'rows_1'=4,'rows_2'=4,'rows_3'=2] {'rows_1'}, use_global_device_ids=true, to_apply=%region_2.3 | all-reduce | flops 2 | bytes 16 | tf_op jit(solution)/shard_map/psum | solution.py:29
  117.4 9.8 %all-reduce.1 = (f32[]{:T(128)}, f32[]{:T(128)}) all-reduce(f32[]{:T(128)} %get-tuple-element.28, f32[]{:T(128)} %get-tuple-element.29), channel_id=1, replica_groups=mesh['rows_0'=4,'rows_1'=4,'rows_2'=4,'rows_3'=2] {'rows_2'}, use_global_device_ids=true, to_apply=%region_3.4 | all-reduce | flops 2 | bytes 16 | tf_op jit(solution)/shard_map/psum | solution.py:29
  127.3 9.4 %all-reduce.7 = (f32[]{:T(128)}, f32[]{:T(128)}) all-reduce(f32[]{:T(128)} %get-tuple-element.24, f32[]{:T(128)} %get-tuple-element.25), channel_id=1, replica_groups=mesh['rows_0'=4,'rows_1'=4,'rows_2'=4,'rows_3'=2] {'rows_3'}, use_global_device_ids=true, to_apply=%region_4.5 | all-reduce | flops 2 | bytes 16 | tf_op jit(solution)/shard_map/psum | solution.py:29
  138.0 1.0 fusion.20
  139.0 6.5 %fusion.6 = f32[128,1,8,9]{3,1,2,0:T(1,128)S(1)} fusion(f32[8,9,9,128]{2,1,0,3:T(8,128)} %copy.71, f32[128,1,9]{2,1,0:T(1,128)S(1)} %fusion.20), kind=kOutput, calls=%fused_computation.23 | convolution fusion | flops 995328 | bytes 373248 | tf_op jit(solution)/shard_map/kabc,ac->bkc/dot_general | solution.py:56
  145.6 2.8 %gather_fusion.6 = f32[1024,9]{1,0:T(8,128)S(1)} fusion(f32[9,1024]{0,1:T(8,128)S(1)} %bitcast.126, s32[1024]{0:T(1024)S(1)} %fusion.12), kind=kCustom, calls=%fused_computation.6 | custom fusion | bytes 77824 | tf_op jit(solution)/shard_map/gather | solution.py:60
  148.4 2.8 %gather_fusion.5 = f32[1024,9]{1,0:T(8,128)S(1)} fusion(f32[9,128]{0,1:T(8,128)S(1)} %bitcast.119, s32[1024]{0:T(1024)S(1)} %broadcast_clamp_fusion), kind=kCustom, calls=%fused_computation.5 | custom fusion | bytes 77824 | tf_op jit(solution)/shard_map/gather | solution.py:59
  151.4 1.1 reshape.212
  152.5 3.7 %all-to-all-start.2 = ((f32[128,1,144]{2,1,0:T(1,128)}), f32[128,1,144]{2,1,0:T(1,128)S(1)}, u32[]{:S(2)}, u32[]{:S(2)}) async-start(f32[128,1,144]{2,1,0:T(1,128)} %reshape.212), calls=%async_computation.2 | async-start | bytes 262144 | tf_op jit(solution)/shard_map/all_to_all | solution.py:20
  156.2 1.0 fusion.8
  157.2 8.9 %all-to-all-done.2 = f32[128,1,144]{2,1,0:T(1,128)S(1)} async-done(((f32[128,1,144]{2,1,0:T(1,128)}), f32[128,1,144]{2,1,0:T(1,128)S(1)}, u32[]{:S(2)}, u32[]{:S(2)}) %all-to-all-start.2) | async-done | bytes 73760 | tf_op jit(solution)/shard_map/all_to_all | solution.py:20
  166.0 1.0 reduce.7
  167.3 2.8 %gather_fusion.7 = f32[1024,9]{1,0:T(8,128)S(1)} fusion(f32[9,1024]{0,1:T(8,128)S(1)} %slice_bitcast_fusion.2, s32[1024]{0:T(1024)S(1)} %fusion.13), kind=kCustom, calls=%fused_computation.7 | custom fusion | bytes 77824 | tf_op jit(solution)/shard_map/gather | solution.py:62
  170.1 9.7 %fusion.2 = f32[128,1,9,1]{2,1,3,0:T(1,128)S(1)} fusion(f32[8,9,9,128]{1,2,0,3:T(8,128)} %copy.74, f32[9,8,128,1]{0,2,1,3:T(8,128)S(1)} %bitcast.131), kind=kOutput, calls=%fused_computation.18 | convolution fusion | flops 995328 | bytes 373248 | tf_op jit(solution)/shard_map/kabc,bkc->ac/dot_general | solution.py:63
  179.8 6.6 %scatter_custom_fusion.1 = f32[9,128]{0,1:T(8,128)S(1)} fusion(f32[9,128]{0,1:T(8,128)S(1)} %add_bitcast_fusion, s32[1024]{0:T(1024)S(1)} %bitcast.142, f32[18,128,8]{0,2,1:T(8,128)S(1)} %bitcast.123), kind=kCustom, calls=%fused_computation.11 | custom fusion | flops 9216 | bytes 528896 | tf_op jit(solution)/shard_map/scatter-add | solution.py:64
  186.4 0.6 multiply_reduce_fusion.1
  187.1 7.5 %all-reduce.4 = (f32[]{:T(128)}, f32[]{:T(128)}) all-reduce(f32[]{:T(128)} %get-tuple-element.19, f32[]{:T(128)} %get-tuple-element.18), channel_id=1, replica_groups=mesh['rows_0'=4,'rows_1'=4,'rows_2'=4,'rows_3'=2] {'rows_0'}, use_global_device_ids=true, to_apply=%region_14.15 | all-reduce | flops 2 | bytes 16 | tf_op jit(solution)/shard_map/psum | solution.py:29
  194.6 7.8 %all-reduce.2 = (f32[]{:T(128)}, f32[]{:T(128)}) all-reduce(f32[]{:T(128)} %get-tuple-element.30, f32[]{:T(128)} %get-tuple-element.31), channel_id=1, replica_groups=mesh['rows_0'=4,'rows_1'=4,'rows_2'=4,'rows_3'=2] {'rows_1'}, use_global_device_ids=true, to_apply=%region_15.16 | all-reduce | flops 2 | bytes 16 | tf_op jit(solution)/shard_map/psum | solution.py:29
  202.4 7.2 %all-reduce = (f32[]{:T(128)}, f32[]{:T(128)}) all-reduce(f32[]{:T(128)} %get-tuple-element.26, f32[]{:T(128)} %get-tuple-element.27), channel_id=1, replica_groups=mesh['rows_0'=4,'rows_1'=4,'rows_2'=4,'rows_3'=2] {'rows_2'}, use_global_device_ids=true, to_apply=%region_16.17 | all-reduce | flops 2 | bytes 16 | tf_op jit(solution)/shard_map/psum | solution.py:29
  209.6 9.2 %all-reduce.6 = (f32[]{:T(128)}, f32[]{:T(128)}) all-reduce(f32[]{:T(128)} %get-tuple-element.22, f32[]{:T(128)} %get-tuple-element.23), channel_id=1, replica_groups=mesh['rows_0'=4,'rows_1'=4,'rows_2'=4,'rows_3'=2] {'rows_3'}, use_global_device_ids=true, to_apply=%region_17.18 | all-reduce | flops 2 | bytes 16 | tf_op jit(solution)/shard_map/psum | solution.py:29
  223.0 0.7 copy.58
  223.7 0.7 copy.59
  (35 shorter events, 2.1 us)
Async XLA Ops:
  0.6 0.8 copy-start
  0.6 28.1 %copy-start.4 = (f32[9,128]{1,0:T(8,128)S(1)}, f32[9,128]{1,0:T(8,128)}, u32[]{:S(2)}) copy-start(f32[9,128]{1,0:T(8,128)} %param.6) | copy-start | bytes 13828
  0.7 28.1 %copy-start.2 = (f32[9,9,128]{2,1,0:T(8,128)S(1)}, f32[9,9,128]{2,1,0:T(8,128)}, u32[]{:S(2)}) copy-start(f32[9,9,128]{2,1,0:T(8,128)} %param.8) | copy-start | bytes 124420
  0.7 28.3 %copy-start.1 = (f32[8,9,9,128]{3,0,2,1:T(8,128)S(1)}, f32[8,9,9,128]{3,0,2,1:T(8,128)}, u32[]{:S(2)}) copy-start(f32[8,9,9,128]{3,0,2,1:T(8,128)} %param.9) | copy-start | bytes 995332
  1.5 35.7 %copy-start.3 = (f32[9,9,128]{2,1,0:T(8,128)S(1)}, f32[9,9,128]{2,1,0:T(8,128)}, u32[]{:S(2)}) copy-start(f32[9,9,128]{2,1,0:T(8,128)} %param.7) | copy-start | bytes 124420
  17.3 35.2 %all-to-all-start = ((s32[128,1,8]{2,1,0:T(1,128)}), s32[128,1,8]{2,1,0:T(1,128)S(1)}, u32[]{:S(2)}, u32[]{:S(2)}) async-start(s32[128,1,8]{2,1,0:T(1,128)} %bitcast.8), calls=%async_computation | async-start | bytes 131072 | tf_op jit(solution)/shard_map/all_to_all | solution.py:45
  58.0 19.5 %all-to-all-start.1 = ((f32[128,1,144]{2,1,0:T(1,128)}), f32[128,1,144]{2,1,0:T(1,128)S(1)}, u32[]{:S(2)}, u32[]{:S(2)}) async-start(f32[128,1,144]{2,1,0:T(1,128)} %reshape.210), calls=%async_computation.1 | async-start | bytes 262144 | tf_op jit(solution)/shard_map/all_to_all | solution.py:20
  152.5 13.6 %all-to-all-start.2 = ((f32[128,1,144]{2,1,0:T(1,128)}), f32[128,1,144]{2,1,0:T(1,128)S(1)}, u32[]{:S(2)}, u32[]{:S(2)}) async-start(f32[128,1,144]{2,1,0:T(1,128)} %reshape.212), calls=%async_computation.2 | async-start | bytes 262144 | tf_op jit(solution)/shard_map/all_to_all | solution.py:20
where the time goes:
time: 225 us; the launch traced here: 224 us
  blocking collectives  68.4 us (30%)
  local copies, waits for them, and re-layouts  52.3 us (23%)
  matrix products  35.5 us (16%)
  other arithmetic  27 us (12%)
  starting transfers between devices  24.9 us (11%)
  waiting for transfers between devices  9.83 us (4%)
  between operations  6.44 us (3%)
    psum x8, blocking collectives, one_axis_at_a_time(): x = lax.psum(x, axis)  68.4 us
    unnamed x21, local copies, waits for them, and re-layouts  21.4 us
    dot_general x2, matrix products, local(): jnp.einsum('kabc,bkc->ac', upper_blocks, gathered, precision=highest)  19.5 us
    all_to_all x2, starting transfers between devices, side_by_side(): lax.all_to_all(both, axis, split_axis=split_dim, concat_axis=concat_dim,...  13.4 us
    dot_general x2, matrix products, local(): jnp.einsum('kabc,ac->bkc', upper_blocks, precond_res, precision=highest)  13 us
    scatter-add x2, other arithmetic, local(): result = result.at[:, requested_flat].add(pushed.reshape(BLOCK, -1))  12.9 us
    all_to_all x1, starting transfers between devices, local(): lax.all_to_all(wanted, ROWS, split_axis=0, concat_axis=0, tiled=True)  11.5 us
    all_to_all x2, waiting for transfers between devices, side_by_side(): lax.all_to_all(both, axis, split_axis=split_dim, concat_axis=concat_dim,...  9.83 us
  transfers between devices with their start and end apart: 3, of which 2 were waited for; matrix products, arithmetic and copies ran while one was open for 15% of the time, Pallas kernels for 0%

commit v1 on v0

v1 whole, which is shorter than its diff:
```python
import functools
import itertools

import jax
import jax.numpy as jnp
from jax import lax
from jax.experimental import pallas as pl
from jax.experimental.pallas import tpu as pltpu
from jax.sharding import PartitionSpec as P

MESH = pl.DeviceIdType.MESH
B = 9
K = 8
N = 128
F32, BF16, I32 = jnp.float32, jnp.bfloat16, jnp.int32


def hops(d):
    return sum(min(k, 4 - k) for k in d[:3])


STEPS = sorted(
    (d for d in itertools.product(range(4), range(4), range(4), range(2)) if any(d)),
    key=lambda d: -hops(d),
)


def targets(me):
    x, y, z, c = me // 32, lax.rem(me // 8, 4), lax.rem(me // 2, 4), lax.rem(me, 2)
    tx = [lax.rem(x + d, 4) * 32 for d in range(4)]
    ty = [lax.rem(y + d, 4) * 8 for d in range(4)]
    tz = [lax.rem(z + d, 4) * 2 for d in range(4)]
    tc = [c, 1 - c]
    xy = {(i, j): tx[i] + ty[j] for i in range(4) for j in range(4)}
    zc = {(i, j): tz[i] + tc[j] for i in range(4) for j in range(2)}
    return [xy[d[0], d[1]] + zc[d[2], d[3]] for d in STEPS]


def iota(shape, dim):
    return lax.broadcasted_iota(I32, shape, dim)


def lanes(x, idx):
    return jnp.take_along_axis(x, idx, axis=1, mode="promise_in_bounds")


def rows8(row):
    return jnp.broadcast_to(row, (K, N))


def pieces(x):
    hi = x.astype(BF16)
    rest = x - hi.astype(F32)
    mid = rest.astype(BF16)
    return hi, mid, (rest - mid.astype(F32)).astype(BF16)


def dot_t(a, b):
    return lax.dot_general(a, b, (((1,), (1,)), ((), ())), preferred_element_type=F32)


def blocks_times(m_ref, v):
    total = m_ref[0] * v[0:1]
    for a in range(1, B):
        total = total + m_ref[a] * v[a : a + 1]
    return total


def kernel(
    b_hbm, d_hbm, p_hbm, u_hbm, c_hbm, t_hbm, x_ref, r_ref,
    b_v, d_v, p_v, u_v, c_v, t_v, in_sem,
    s0, m0, s1, m1, s2, m2, s3, m3, send, recv, pt, ft,
):
    me = lax.axis_index("rows")
    peers = targets(me)
    barrier = pltpu.get_barrier_semaphore()
    for t in peers:
        pl.semaphore_signal(barrier, inc=1, device_id=(t,), device_id_type=MESH)
    copies = [
        pltpu.make_async_copy(src, dst, in_sem.at[i])
        for i, (src, dst) in enumerate(
            [(c_hbm, c_v), (t_hbm, t_v), (b_hbm, b_v), (p_hbm, p_v), (u_hbm, u_v), (d_hbm, d_v)]
        )
    ]
    for c in copies:
        c.start()

    def exchange(n, src, dst, one=False):
        for t in peers:
            pltpu.make_async_remote_copy(
                src_ref=src.at[0 if one else t],
                dst_ref=dst.at[me],
                send_sem=send.at[n],
                recv_sem=recv.at[n],
                device_id=(t,),
                device_id_type=MESH,
            ).start()
        dst[me] = src[0] if one else src[me]

    def arrived(n, dst):
        pltpu.make_async_copy(dst.at[0 : N - 1], dst.at[0 : N - 1], recv.at[n]).wait()

    copies[0].wait()
    copies[1].wait()
    cams = c_v[...]
    hi, lo = cams >> 7, cams & 127
    slots = jnp.zeros((K, N), I32)
    for r in range(N):
        slots = jnp.where(hi == r, lanes(rows8(t_v[r : r + 1, :]), lo), slots)
    owner, offset = slots >> 7, slots & 127

    sub = iota((N, N), 0)
    picks = [sub == owner[k : k + 1, :] for k in range(K)]
    ones = [jnp.where(p, 1.0, 0.0).astype(BF16) for p in picks]
    by_owner = jnp.concatenate(ones, axis=1)
    before = jnp.where(sub < iota((N, N), 1), 1.0, 0.0).astype(BF16)
    stacked = jnp.concatenate(ones, axis=0)
    earlier = jnp.dot(stacked, before, preferred_element_type=F32)
    counts = jnp.dot(stacked, jnp.ones((N, N), BF16), preferred_element_type=F32)
    base = jnp.zeros((N, N), F32)
    ranks = []
    for k in range(K):
        here = earlier[k * N : (k + 1) * N] + base
        ranks.append(jnp.sum(jnp.where(picks[k], here, 0.0), axis=0, keepdims=True))
        base = base + counts[k * N : (k + 1) * N]
    rank = jnp.concatenate(ranks, axis=0).astype(I32)
    sub8 = iota((K, N), 0)
    places = [rank[k : k + 1, :] == sub8 for k in range(K)]

    def spread(v):
        out = []
        for b in range(B):
            total = u_v[0, b] * v[0:1]
            for a in range(1, B):
                total = total + u_v[a, b] * v[a : a + 1]
            out.append(total)
        return out

    def to_owners(lists):
        wide = jnp.concatenate(
            [
                jnp.concatenate(
                    [jnp.where(places[k], rows8(e[k : k + 1, :]), 0.0) for k in range(K)], axis=1
                )
                for e in lists
            ]
            + [jnp.zeros((N - K * len(lists), K * N), F32)],
            axis=0,
        )
        h, m, l = pieces(wide)
        return dot_t(by_owner, h) + dot_t(by_owner, m) + dot_t(by_owner, l)

    def answers(v, asked):
        parts = [lanes(rows8(v[b : b + 1]), asked) for b in range(B)]
        return jnp.concatenate(parts + [jnp.zeros((N - K * B, N), F32)], axis=0).T

    def scatter(got, onehot):
        pt[...] = got[0 : K * B]
        flat = jnp.concatenate([pt[pl.ds(r, B, stride=K), :] for r in range(K)], axis=1)
        h, m, l = pieces(flat)
        return dot_t(h, onehot) + dot_t(m, onehot) + dot_t(l, onehot)

    def forward(got):
        ft[...] = got[0 : K * B]
        total = [jnp.zeros((K, N), F32) for _ in range(B)]
        for b in range(B):
            g = jnp.zeros((K, N), F32)
            for r in range(K):
                row = rows8(ft[K * b + r : K * b + r + 1, :])
                g = jnp.where(rank == r, lanes(row, owner), g)
            for a in range(B):
                total[a] = total[a] + u_v[a, b] * g
        return jnp.concatenate([jnp.sum(t, axis=0, keepdims=True) for t in total], axis=0)

    copies[2].wait()
    copies[3].wait()
    rhs = b_v[...]
    z0 = blocks_times(p_v, rhs)
    copies[4].wait()
    copies[5].wait()
    s0[:, 0, :] = to_owners(spread(z0) + [offset.astype(F32)])
    pl.semaphore_wait(barrier, N - 1)
    exchange(0, s0, m0)

    lane = iota((N, N), 1)
    partial = blocks_times(d_v, z0)
    rho0_part = jnp.sum(rhs * z0)
    arrived(0, m0)
    got = m0[:, 0, :].T
    asked = got[K * B : K * B + K].astype(I32)
    s1[:, 0, :] = answers(z0, asked)
    exchange(1, s1, m1)
    onehot = jnp.concatenate(
        [jnp.where(sub == asked[r : r + 1, :], 1.0, 0.0).astype(BF16) for r in range(K)], axis=1
    )
    partial = partial + scatter(got, onehot)
    arrived(1, m1)
    q0 = partial + forward(m1[:, 0, :].T)

    w0 = blocks_times(p_v, q0)
    c0_part = jnp.sum(z0 * q0)
    out = to_owners(spread(w0))
    s2[:, 0, :] = jnp.where(lane == 80, rho0_part, jnp.where(lane == 81, c0_part, out))
    s2[:, 1, :] = answers(w0, asked)
    exchange(2, s2, m2)
    partial = blocks_times(d_v, w0)
    arrived(2, m2)
    first = m2[:, 0, :]
    sums = jnp.sum(first, axis=0, keepdims=True)
    lane1 = iota((1, N), 1)
    rho0 = jnp.sum(jnp.where(lane1 == 80, sums, 0.0))
    c0 = jnp.sum(jnp.where(lane1 == 81, sums, 0.0))
    alpha = jnp.full((1, 1), rho0, F32) / jnp.full((1, 1), c0, F32)
    image = partial + scatter(first.T, onehot) + forward(m2[:, 1, :].T)

    r1 = rhs - alpha * q0
    z1 = z0 - alpha * w0
    y1 = q0 - alpha * image
    rho1_part, c1_part, e1_part = jnp.sum(r1 * z1), jnp.sum(z1 * y1), jnp.sum(z1 * q0)
    s3[0] = jnp.where(
        lane1 == 0, rho1_part, jnp.where(lane1 == 1, c1_part, jnp.where(lane1 == 2, e1_part, 0.0))
    )
    exchange(3, s3, m3, one=True)
    arrived(3, m3)
    sums = jnp.sum(m3[:, 0, :], axis=0, keepdims=True)
    rho1, c1, e1 = (
        jnp.full((1, 1), jnp.sum(jnp.where(lane1 == i, sums, 0.0)), F32) for i in range(3)
    )
    beta = rho1 / jnp.full((1, 1), rho0, F32)
    step = rho1 / (c1 + 2.0 * beta * e1 + beta * beta * jnp.full((1, 1), c0, F32))
    x_ref[...] = alpha * z0 + step * (z1 + beta * z0)
    r_ref[...] = r1 - step * (y1 + beta * q0)
    for n, src in ((0, s0), (1, s1), (2, s2), (3, m3)):
        pltpu.make_async_copy(src.at[0 : N - 1], src.at[0 : N - 1], send.at[n]).wait()


def solve(right_side, diag_blocks, precond, upper_blocks, block_cols, slot_of_camera):
    shape = jax.ShapeDtypeStruct((B, N), F32)
    any_space = pl.BlockSpec(memory_space=pl.ANY)
    vmem = pl.BlockSpec(memory_space=pltpu.VMEM)
    row, two = pltpu.VMEM((N, 1, N), F32), pltpu.VMEM((N, 2, N), F32)
    return pl.pallas_call(
        kernel,
        out_shape=(shape, shape),
        in_specs=[any_space] * 6,
        out_specs=(vmem, vmem),
        scratch_shapes=[
            pltpu.VMEM((B, N), F32),
            pltpu.VMEM((B, B, N), F32),
            pltpu.VMEM((B, B, N), F32),
            pltpu.VMEM((B, B, K, N), F32),
            pltpu.VMEM((K, N), I32),
            pltpu.VMEM((N, N), I32),
            pltpu.SemaphoreType.DMA((6,)),
            row, row, row, row, two, two, pltpu.VMEM((1, 1, N), F32), row,
            pltpu.SemaphoreType.DMA((4,)),
            pltpu.SemaphoreType.DMA((4,)),
            pltpu.VMEM((K * B, N), F32),
            pltpu.VMEM((K * B, N), F32),
        ],
        compiler_params=pltpu.CompilerParams(collective_id=0, has_side_effects=True),
    )(
        right_side,
        diag_blocks,
        precond,
        jnp.transpose(upper_blocks, (1, 2, 0, 3)),
        block_cols,
        slot_of_camera.reshape(N, N),
    )


def solution(mesh):
    return jax.shard_map(
        solve,
        mesh=mesh,
        in_specs=(
            P(None, "rows"),
            P(None, None, "rows"),
            P(None, None, "rows"),
            P(None, None, None, "rows"),
            P(None, "rows"),
            P(),
        ),
        out_specs=(P(None, "rows"), P(None, "rows")),
        check_vma=False,
    )
```

time: 225 us -> 38.8 us (0.17)
  blocking collectives: 68.4 us -> 0 us
  local copies, waits for them, and re-layouts: 52.3 us -> 1.9 us
  Pallas kernels: 0 us -> 36.1 us
  matrix products: 35.5 us -> 0 us
  other arithmetic: 27 us -> 0 us
  starting transfers between devices: 24.9 us -> 0 us
  waiting for transfers between devices: 9.83 us -> 0 us
  between operations: 6.44 us -> 0.65 us
    psum x8 -> x0, blocking collectives: 68.4 us -> none  [one_axis_at_a_time(): x = lax.psum(x, axis)]
    pallas_call x0 -> x1, Pallas kernels: none -> 36.1 us  [solve(): pl.pallas_call(kernel, out_shape=(shape, shape), in_specs=[any_space] * 6...]
    dot_general x7 -> x0, matrix products: 35.5 us -> none  [the longest x2 19.5 us: local(): jnp.einsum('kabc,bkc->ac', upper_blocks, gathered, precision=highest)]
    gather x8 -> x0, local copies, waits for them, and re-layouts: 28.7 us -> none  [the longest x2 6.81 us: local(): fetched.reshape(BLOCK, -1)[:, inverse_order]]
    all_to_all x3 -> x0, starting transfers between devices: 24.9 us -> none  [the longest x2 13.4 us: side_by_side(): lax.all_to_all(both, axis, split_axis=split_dim, concat_axis=concat_dim,...]
    unnamed x21 -> x4, local copies, waits for them, and re-layouts: 21.4 us -> 1.9 us
    scatter-add x2 -> x0, other arithmetic: 12.9 us -> none  [local(): result = result.at[:, requested_flat].add(pushed.reshape(BLOCK, -1))]
    all_to_all x3 -> x0, waiting for transfers between devices: 9.83 us -> none  [the longest x2 9.83 us: side_by_side(): lax.all_to_all(both, axis, split_axis=split_dim, concat_axis=concat_dim,...]
  transfers between devices with their start and end apart: 3 -> 0, of which waited for: 2 -> 0; matrix products, arithmetic and copies ran while one was open for 15% -> 0% of each run, Pallas kernels for 0% -> 0%
where the time goes in v1:
time: 38.8 us; the launch traced here: 38.6 us
  Pallas kernels  36.1 us (93%)
  local copies, waits for them, and re-layouts  1.9 us (5%)
  between operations  0.65 us (2%)
    pallas_call x1, Pallas kernels, solve(): pl.pallas_call(kernel, out_shape=(shape, shape), in_specs=[any_space] * 6...  36.1 us
    unnamed x4, local copies, waits for them, and re-layouts  1.9 us

profile of v1, /device:TPU:1, one launch (start us, length us, event | category | flops | bytes accessed | tf_op | source)
XLA Modules:
  0.0 38.6 jit_solution(9243606834327017899)
XLA Ops:
  0.6 36.1 %shard_map.77 = (f32[9,128]{1,0:T(8,128)}, f32[9,128]{1,0:T(8,128)}) custom-call(f32[9,128]{1,0:T(8,128)} %b_hbm.1, f32[9,9,128]{2,1,0:T(8,128)} %d_hbm.1, f32[9,9,128]{2,1,0:T(8,128)} %p_hbm.1, f32[9,9,8,128]{3,2,1,0:T(8,128)} %bitcast.2, s32[8,128]{1,0:T(8,128)} %c_hbm.1, s32[128,128]{1,0:T(8,128)} %bitcast.3), custom_call_target="tpu_custom_call" | custom-call | tf_op jit(solution)/shard_map/pallas_call | solution.py:242
  36.7 0.0 copy-start
  36.7 1.3 %copy.10 = f32[9,128]{1,0:T(8,128)} copy(f32[9,128]{1,0:T(8,128)} %get-tuple-element.4) | data formatting | bytes 9216
  38.0 0.0 copy-done
  38.0 0.6 %copy.11 = f32[9,128]{1,0:T(8,128)} copy(f32[9,128]{1,0:T(8,128)S(1)} %copy-done) | data formatting | bytes 9216
Async XLA Ops:
  36.7 1.3 %copy-start = (f32[9,128]{1,0:T(8,128)S(1)}, f32[9,128]{1,0:T(8,128)}, u32[]{:S(2)}) copy-start(f32[9,128]{1,0:T(8,128)} %get-tuple-element.5) | copy-start | bytes 13828

commit v2 on v1

--- a/solution.py
+++ b/solution.py
@@ -67,7 +67,7 @@
 
 
 def kernel(
-    b_hbm, d_hbm, p_hbm, u_hbm, c_hbm, t_hbm, x_ref, r_ref,
+    b_hbm, d_hbm, p_hbm, u_hbm, c_hbm, t_hbm, o_ref,
     b_v, d_v, p_v, u_v, c_v, t_v, in_sem,
     s0, m0, s1, m1, s2, m2, s3, m3, send, recv, pt, ft,
 ):
@@ -228,22 +228,22 @@
     )
     beta = rho1 / jnp.full((1, 1), rho0, F32)
     step = rho1 / (c1 + 2.0 * beta * e1 + beta * beta * jnp.full((1, 1), c0, F32))
-    x_ref[...] = alpha * z0 + step * (z1 + beta * z0)
-    r_ref[...] = r1 - step * (y1 + beta * q0)
+    o_ref[0] = alpha * z0 + step * (z1 + beta * z0)
+    o_ref[1] = r1 - step * (y1 + beta * q0)
     for n, src in ((0, s0), (1, s1), (2, s2), (3, m3)):
         pltpu.make_async_copy(src.at[0 : N - 1], src.at[0 : N - 1], send.at[n]).wait()
 
 
 def solve(right_side, diag_blocks, precond, upper_blocks, block_cols, slot_of_camera):
     shape = jax.ShapeDtypeStruct((B, N), F32)
-    any_space = pl.BlockSpec(memory_space=pl.ANY)
+    any_space = pl.BlockSpec(memory_space=pltpu.HBM)
     vmem = pl.BlockSpec(memory_space=pltpu.VMEM)
     row, two = pltpu.VMEM((N, 1, N), F32), pltpu.VMEM((N, 2, N), F32)
-    return pl.pallas_call(
+    out = pl.pallas_call(
         kernel,
-        out_shape=(shape, shape),
+        out_shape=jax.ShapeDtypeStruct((2, B, N), F32),
         in_specs=[any_space] * 6,
-        out_specs=(vmem, vmem),
+        out_specs=vmem,
         scratch_shapes=[
             pltpu.VMEM((B, N), F32),
             pltpu.VMEM((B, B, N), F32),
@@ -258,15 +258,21 @@
             pltpu.VMEM((K * B, N), F32),
             pltpu.VMEM((K * B, N), F32),
         ],
-        compiler_params=pltpu.CompilerParams(collective_id=0, has_side_effects=True),
+        compiler_params=pltpu.CompilerParams(collective_id=0, has_side_effects=True, vmem_limit_bytes=8 << 20),
     )(
-        right_side,
-        diag_blocks,
-        precond,
-        jnp.transpose(upper_blocks, (1, 2, 0, 3)),
-        block_cols,
-        slot_of_camera.reshape(N, N),
-    )
+        *[
+            pltpu.with_memory_space_constraint(x, pltpu.HBM)
+            for x in (
+                right_side,
+                diag_blocks,
+                precond,
+                jnp.transpose(upper_blocks, (1, 2, 0, 3)),
+                block_cols,
+                slot_of_camera.reshape(N, N),
+            )
+        ]
+    )
+    return out[0], out[1]
 
 
 def solution(mesh):

time: 38.8 us -> 36.8 us (0.948)
  local copies, waits for them, and re-layouts: 1.9 us -> 0.61 us
  Pallas kernels: 36.1 us -> 35.5 us
    unnamed x4 -> x0, local copies, waits for them, and re-layouts: 1.9 us -> none
    squeeze x0 -> x1, local copies, waits for them, and re-layouts: none -> 0.61 us  [solve(): return (out[0], out[1])]
    pallas_call x1, Pallas kernels: 36.1 us -> 35.5 us  [solve(): pl.pallas_call(kernel, out_shape=jax.ShapeDtypeStruct((2, B, N), F32), in...]
where the time goes in v2:
time: 36.8 us; the launch traced here: 36.7 us
  Pallas kernels  35.5 us (96%)
  between operations  0.64 us (2%)
  local copies, waits for them, and re-layouts  0.61 us (2%)
    pallas_call x1, Pallas kernels, solve(): pl.pallas_call(kernel, out_shape=jax.ShapeDtypeStruct((2, B, N), F32), in...  35.5 us

profile of v2, /device:TPU:1, one launch (start us, length us, event | category | flops | bytes accessed | tf_op | source)
XLA Modules:
  0.0 36.7 jit_solution(5077110346051151751)
XLA Ops:
  0.6 35.5 %shard_map.77 = f32[2,9,128]{2,1,0:T(8,128)S(1)} custom-call(f32[9,128]{1,0:T(8,128)} %b_hbm.1, f32[9,9,128]{2,1,0:T(8,128)} %d_hbm.1, f32[9,9,128]{2,1,0:T(8,128)} %p_hbm.1, f32[9,9,8,128]{3,2,1,0:T(8,128)} %bitcast.6, s32[8,128]{1,0:T(8,128)} %c_hbm.1, s32[128,128]{1,0:T(8,128)} %bitcast.7), custom_call_target="tpu_custom_call" | custom-call | tf_op jit(solution)/shard_map/pallas_call | solution.py:242
  36.1 0.6 %slice_bitcast_fusion = (f32[9,128]{1,0:T(8,128)}, f32[9,128]{1,0:T(8,128)}) fusion(f32[2,9,128]{2,1,0:T(8,128)S(1)} %shard_map.77), kind=kLoop, calls=%fused_computation | loop fusion | bytes 18432 | tf_op jit(solution)/shard_map/squeeze | solution.py:275

commit v3 on v2

--- a/solution.py
+++ b/solution.py
@@ -12,6 +12,8 @@
 B = 9
 K = 8
 N = 128
+CHIPS = N // 2
+PLANE = 16
 F32, BF16, I32 = jnp.float32, jnp.bfloat16, jnp.int32
 
 
@@ -33,7 +35,11 @@
     tc = [c, 1 - c]
     xy = {(i, j): tx[i] + ty[j] for i in range(4) for j in range(4)}
     zc = {(i, j): tz[i] + tc[j] for i in range(4) for j in range(2)}
-    return [xy[d[0], d[1]] + zc[d[2], d[3]] for d in STEPS]
+    return {d: xy[d[0], d[1]] + zc[d[2], d[3]] for d in STEPS}
+
+
+def place_of(device):
+    return lax.rem(device, 2) * CHIPS + device // 2
 
 
 def iota(shape, dim):
@@ -69,13 +75,12 @@
 def kernel(
     b_hbm, d_hbm, p_hbm, u_hbm, c_hbm, t_hbm, o_ref,
     b_v, d_v, p_v, u_v, c_v, t_v, in_sem,
-    s0, m0, s1, m1, s2, m2, s3, m3, send, recv, pt, ft,
+    s0, m0, tile, tiles, s2, m2, s3, m3, send, recv, plane_recv, half_send, half_recv, pt, ft, wt, gt,
 ):
     me = lax.axis_index("rows")
+    mine = place_of(me)
+    core = lax.rem(me, 2)
     peers = targets(me)
-    barrier = pltpu.get_barrier_semaphore()
-    for t in peers:
-        pl.semaphore_signal(barrier, inc=1, device_id=(t,), device_id_type=MESH)
     copies = [
         pltpu.make_async_copy(src, dst, in_sem.at[i])
         for i, (src, dst) in enumerate(
@@ -84,21 +89,28 @@
     ]
     for c in copies:
         c.start()
+    barrier = pltpu.get_barrier_semaphore()
+    for d in STEPS:
+        pl.semaphore_signal(barrier, inc=1, device_id=(peers[d],), device_id_type=MESH)
 
     def exchange(n, src, dst, one=False):
-        for t in peers:
+        for d in STEPS:
             pltpu.make_async_remote_copy(
-                src_ref=src.at[0 if one else t],
-                dst_ref=dst.at[me],
+                src_ref=src.at[0 if one else place_of(peers[d])],
+                dst_ref=dst.at[mine],
                 send_sem=send.at[n],
                 recv_sem=recv.at[n],
-                device_id=(t,),
+                device_id=(peers[d],),
                 device_id_type=MESH,
             ).start()
-        dst[me] = src[0] if one else src[me]
+        dst[mine] = src[0] if one else src[mine]
 
     def arrived(n, dst):
         pltpu.make_async_copy(dst.at[0 : N - 1], dst.at[0 : N - 1], recv.at[n]).wait()
+
+    def plane(dx, half):
+        x = lax.rem(me // 32 - dx + 4, 4)
+        return pl.ds(pl.multiple_of(half * CHIPS + x * PLANE, PLANE), PLANE)
 
     copies[0].wait()
     copies[1].wait()
@@ -107,7 +119,8 @@
     slots = jnp.zeros((K, N), I32)
     for r in range(N):
         slots = jnp.where(hi == r, lanes(rows8(t_v[r : r + 1, :]), lo), slots)
-    owner, offset = slots >> 7, slots & 127
+    device, offset = slots >> 7, slots & 127
+    owner = (device & 1) * CHIPS + (device >> 1)
 
     sub = iota((N, N), 0)
     picks = [sub == owner[k : k + 1, :] for k in range(K)]
@@ -176,26 +189,77 @@
     copies[3].wait()
     rhs = b_v[...]
     z0 = blocks_times(p_v, rhs)
+    tile[:, 0, :] = z0
     copies[4].wait()
     copies[5].wait()
     s0[:, 0, :] = to_owners(spread(z0) + [offset.astype(F32)])
+    wanted = jnp.concatenate(
+        [jnp.where(places[k], rows8(offset[k : k + 1, :]), 0).astype(F32) for k in range(K)], axis=1
+    )
+    wanted = jnp.concatenate([wanted] * (N // K), axis=0).astype(BF16)
+    wanted = dot_t(by_owner, wanted).astype(I32)
     pl.semaphore_wait(barrier, N - 1)
+
+    for dx in (2, 1, 3, 0):
+        for d in STEPS:
+            if d[0] == dx and d[3] == 0:
+                pltpu.make_async_remote_copy(
+                    src_ref=tile,
+                    dst_ref=tiles.at[:, mine],
+                    send_sem=send.at[1],
+                    recv_sem=plane_recv.at[dx],
+                    device_id=(peers[d],),
+                    device_id_type=MESH,
+                ).start()
     exchange(0, s0, m0)
+    tiles[:, mine] = tile[...]
 
     lane = iota((N, N), 1)
     partial = blocks_times(d_v, z0)
     rho0_part = jnp.sum(rhs * z0)
+    halves = []
+    for dx in (0, 1, 3, 2):
+        n = PLANE - (dx == 0)
+        pltpu.make_async_copy(tiles.at[:, 0:n], tiles.at[:, 0:n], plane_recv.at[dx]).wait()
+        here = tiles.at[:, plane(dx, core)]
+        halves.append(
+            pltpu.make_async_remote_copy(
+                src_ref=here,
+                dst_ref=here,
+                send_sem=half_send.at[dx],
+                recv_sem=half_recv.at[dx],
+                device_id=(peers[0, 0, 0, 1],),
+                device_id_type=MESH,
+            )
+        )
+        halves[-1].start()
+
+    block = iota((PLANE, N), 1) >> 3
+    wt[...] = wanted
+
+    def pick(dx, half):
+        where = plane(dx, half)
+        index = wt[where, :]
+        out = jnp.zeros((PLANE, N), F32)
+        for b in range(B):
+            z = tiles[b, where, 0, :]
+            g = jnp.concatenate([lanes(z[i : i + K], index[i : i + K]) for i in (0, K)], axis=0)
+            out = jnp.where(block == b, g, out)
+        gt[where, :] = out
+
+    for dx in (0, 1, 3, 2):
+        pick(dx, core)
     arrived(0, m0)
     got = m0[:, 0, :].T
     asked = got[K * B : K * B + K].astype(I32)
-    s1[:, 0, :] = answers(z0, asked)
-    exchange(1, s1, m1)
     onehot = jnp.concatenate(
         [jnp.where(sub == asked[r : r + 1, :], 1.0, 0.0).astype(BF16) for r in range(K)], axis=1
     )
     partial = partial + scatter(got, onehot)
-    arrived(1, m1)
-    q0 = partial + forward(m1[:, 0, :].T)
+    for n, dx in enumerate((0, 1, 3, 2)):
+        halves[n].wait_recv()
+        pick(dx, 1 - core)
+    q0 = partial + forward(gt[...].T)
 
     w0 = blocks_times(p_v, q0)
     c0_part = jnp.sum(z0 * q0)
@@ -230,8 +294,13 @@
     step = rho1 / (c1 + 2.0 * beta * e1 + beta * beta * jnp.full((1, 1), c0, F32))
     o_ref[0] = alpha * z0 + step * (z1 + beta * z0)
     o_ref[1] = r1 - step * (y1 + beta * q0)
-    for n, src in ((0, s0), (1, s1), (2, s2), (3, m3)):
+    for n, src in ((0, m0), (2, m2), (3, m3)):
         pltpu.make_async_copy(src.at[0 : N - 1], src.at[0 : N - 1], send.at[n]).wait()
+    pltpu.make_async_copy(
+        tiles.at[:, 0 : CHIPS - 1], tiles.at[:, 0 : CHIPS - 1], send.at[1]
+    ).wait()
+    for h in halves:
+        h.wait_send()
 
 
 def solve(right_side, diag_blocks, precond, upper_blocks, block_cols, slot_of_camera):
@@ -252,11 +321,13 @@
             pltpu.VMEM((K, N), I32),
             pltpu.VMEM((N, N), I32),
             pltpu.SemaphoreType.DMA((6,)),
-            row, row, row, row, two, two, pltpu.VMEM((1, 1, N), F32), row,
-            pltpu.SemaphoreType.DMA((4,)),
-            pltpu.SemaphoreType.DMA((4,)),
+            row, row, pltpu.VMEM((B, 1, N), F32), pltpu.VMEM((B, N, 1, N), F32),
+            two, two, pltpu.VMEM((1, 1, N), F32), row,
+            *[pltpu.SemaphoreType.DMA((4,))] * 5,
             pltpu.VMEM((K * B, N), F32),
             pltpu.VMEM((K * B, N), F32),
+            pltpu.VMEM((N, N), I32),
+            pltpu.VMEM((N, N), F32),
         ],
         compiler_params=pltpu.CompilerParams(collective_id=0, has_side_effects=True, vmem_limit_bytes=8 << 20),
     )(

time: 36.8 us -> 34.1 us (0.927)
  Pallas kernels: 35.5 us -> 32.7 us
    pallas_call x1, Pallas kernels: 35.5 us -> 32.7 us  [solve(): pl.pallas_call(kernel, out_shape=jax.ShapeDtypeStruct((2, B, N), F32), in...]
where the time goes in v3:
time: 34.1 us; the launch traced here: 34 us
  Pallas kernels  32.7 us (96%)
  between operations  0.64 us (2%)
  local copies, waits for them, and re-layouts  0.61 us (2%)
    pallas_call x1, Pallas kernels, solve(): pl.pallas_call(kernel, out_shape=jax.ShapeDtypeStruct((2, B, N), F32), in...  32.7 us

profile of v3, /device:TPU:1, one launch (start us, length us, event | category | flops | bytes accessed | tf_op | source)
XLA Modules:
  0.0 34.0 jit_solution(2543159580222971958)
XLA Ops:
  0.6 32.7 %shard_map.77 = f32[2,9,128]{2,1,0:T(8,128)S(1)} custom-call(f32[9,128]{1,0:T(8,128)} %b_hbm.1, f32[9,9,128]{2,1,0:T(8,128)} %d_hbm.1, f32[9,9,128]{2,1,0:T(8,128)} %p_hbm.1, f32[9,9,8,128]{3,2,1,0:T(8,128)} %bitcast.6, s32[8,128]{1,0:T(8,128)} %c_hbm.1, s32[128,128]{1,0:T(8,128)} %bitcast.7), custom_call_target="tpu_custom_call" | custom-call | tf_op jit(solution)/shard_map/pallas_call | solution.py:311
  33.4 0.6 %slice_bitcast_fusion = (f32[9,128]{1,0:T(8,128)}, f32[9,128]{1,0:T(8,128)}) fusion(f32[2,9,128]{2,1,0:T(8,128)S(1)} %shard_map.77), kind=kLoop, calls=%fused_computation | loop fusion | bytes 18432 | tf_op jit(solution)/shard_map/squeeze | solution.py:346

commit v4 on v3

--- a/solution.py
+++ b/solution.py
@@ -27,15 +27,22 @@
 )
 
 
-def targets(me):
-    x, y, z, c = me // 32, lax.rem(me // 8, 4), lax.rem(me // 2, 4), lax.rem(me, 2)
-    tx = [lax.rem(x + d, 4) * 32 for d in range(4)]
-    ty = [lax.rem(y + d, 4) * 8 for d in range(4)]
-    tz = [lax.rem(z + d, 4) * 2 for d in range(4)]
-    tc = [c, 1 - c]
-    xy = {(i, j): tx[i] + ty[j] for i in range(4) for j in range(4)}
-    zc = {(i, j): tz[i] + tc[j] for i in range(4) for j in range(2)}
-    return {d: xy[d[0], d[1]] + zc[d[2], d[3]] for d in STEPS}
+class Peers:
+    def __init__(self, me):
+        x, y, z, c = me // 32, lax.rem(me // 8, 4), lax.rem(me // 2, 4), lax.rem(me, 2)
+        self.x = [lax.rem(x + d, 4) * 16 for d in range(4)]
+        self.yz = [[lax.rem(y + i, 4) * 4 + lax.rem(z + j, 4) for j in range(4)] for i in range(4)]
+        self.core = [c, 1 - c]
+        self.half = [c * CHIPS, CHIPS - c * CHIPS]
+
+    def chip(self, d):
+        return self.x[d[0]] + self.yz[d[1]][d[2]]
+
+    def device(self, d):
+        return self.chip(d) * 2 + self.core[d[3]]
+
+    def place(self, d):
+        return self.chip(d) + self.half[d[3]]
 
 
 def place_of(device):
@@ -59,6 +66,11 @@
     rest = x - hi.astype(F32)
     mid = rest.astype(BF16)
     return hi, mid, (rest - mid.astype(F32)).astype(BF16)
+
+
+def total(x):
+    rows = jnp.sum(x, axis=0, keepdims=True)
+    return jnp.sum(rows, axis=1, keepdims=True)
 
 
 def dot_t(a, b):
@@ -80,7 +92,17 @@
     me = lax.axis_index("rows")
     mine = place_of(me)
     core = lax.rem(me, 2)
-    peers = targets(me)
+    peers = Peers(me)
+    barrier = pltpu.get_barrier_semaphore()
+
+    def greet(steps):
+        for d in steps:
+            pl.semaphore_signal(
+                barrier, inc=1, device_id=(peers.device(d),), device_id_type=MESH
+            )
+
+    far = [d for d in STEPS if hops(d) > 4]
+    greet(far)
     copies = [
         pltpu.make_async_copy(src, dst, in_sem.at[i])
         for i, (src, dst) in enumerate(
@@ -89,24 +111,27 @@
     ]
     for c in copies:
         c.start()
-    barrier = pltpu.get_barrier_semaphore()
-    for d in STEPS:
-        pl.semaphore_signal(barrier, inc=1, device_id=(peers[d],), device_id_type=MESH)
-
-    def exchange(n, src, dst, one=False):
+    greet(STEPS[len(far) :])
+
+    def exchange(n, src, dst, rows=1, one=False):
+        def of(ref, place):
+            return ref.at[pl.ds(place * rows, rows)]
+
         for d in STEPS:
             pltpu.make_async_remote_copy(
-                src_ref=src.at[0 if one else place_of(peers[d])],
-                dst_ref=dst.at[mine],
+                src_ref=src if one else of(src, peers.place(d)),
+                dst_ref=of(dst, mine),
                 send_sem=send.at[n],
                 recv_sem=recv.at[n],
-                device_id=(peers[d],),
+                device_id=(peers.device(d),),
                 device_id_type=MESH,
             ).start()
-        dst[mine] = src[0] if one else src[mine]
-
-    def arrived(n, dst):
-        pltpu.make_async_copy(dst.at[0 : N - 1], dst.at[0 : N - 1], recv.at[n]).wait()
+        own = pl.ds(mine * rows, rows)
+        dst[own, :] = src[...] if one else src[own, :]
+
+    def arrived(n, dst, rows=1):
+        most = dst.at[0 : rows * (N - 1)]
+        pltpu.make_async_copy(most, most, recv.at[n]).wait()
 
     def plane(dx, half):
         x = lax.rem(me // 32 - dx + 4, 4)
@@ -161,17 +186,18 @@
             axis=0,
         )
         h, m, l = pieces(wide)
-        return dot_t(by_owner, h) + dot_t(by_owner, m) + dot_t(by_owner, l)
+        both = dot_t(by_owner, jnp.concatenate([h, m], axis=0))
+        return both[:, 0:N] + both[:, N:] + dot_t(by_owner, l)
 
     def answers(v, asked):
         parts = [lanes(rows8(v[b : b + 1]), asked) for b in range(B)]
         return jnp.concatenate(parts + [jnp.zeros((N - K * B, N), F32)], axis=0).T
 
     def scatter(got, onehot):
-        pt[...] = got[0 : K * B]
-        flat = jnp.concatenate([pt[pl.ds(r, B, stride=K), :] for r in range(K)], axis=1)
-        h, m, l = pieces(flat)
-        return dot_t(h, onehot) + dot_t(m, onehot) + dot_t(l, onehot)
+        pt[...] = got
+        flat = jnp.concatenate([pt[pl.ds(r, 16, stride=K), :] for r in range(K)], axis=1)
+        out = dot_t(jnp.concatenate(pieces(flat), axis=0), onehot)
+        return out[0:B] + out[16 : 16 + B] + out[32 : 32 + B]
 
     def forward(got):
         ft[...] = got[0 : K * B]
@@ -189,10 +215,10 @@
     copies[3].wait()
     rhs = b_v[...]
     z0 = blocks_times(p_v, rhs)
-    tile[:, 0, :] = z0
+    tile[...] = z0
     copies[4].wait()
     copies[5].wait()
-    s0[:, 0, :] = to_owners(spread(z0) + [offset.astype(F32)])
+    s0[...] = to_owners(spread(z0) + [offset.astype(F32)])
     wanted = jnp.concatenate(
         [jnp.where(places[k], rows8(offset[k : k + 1, :]), 0).astype(F32) for k in range(K)], axis=1
     )
@@ -208,7 +234,7 @@
                     dst_ref=tiles.at[:, mine],
                     send_sem=send.at[1],
                     recv_sem=plane_recv.at[dx],
-                    device_id=(peers[d],),
+                    device_id=(peers.device(d),),
                     device_id_type=MESH,
                 ).start()
     exchange(0, s0, m0)
@@ -216,7 +242,7 @@
 
     lane = iota((N, N), 1)
     partial = blocks_times(d_v, z0)
-    rho0_part = jnp.sum(rhs * z0)
+    rho0_part = total(rhs * z0)
     halves = []
     for dx in (0, 1, 3, 2):
         n = PLANE - (dx == 0)
@@ -228,7 +254,7 @@
                 dst_ref=here,
                 send_sem=half_send.at[dx],
                 recv_sem=half_recv.at[dx],
-                device_id=(peers[0, 0, 0, 1],),
+                device_id=(peers.device((0, 0, 0, 1)),),
                 device_id_type=MESH,
             )
         )
@@ -242,7 +268,7 @@
         index = wt[where, :]
         out = jnp.zeros((PLANE, N), F32)
         for b in range(B):
-            z = tiles[b, where, 0, :]
+            z = tiles[b, where, :]
             g = jnp.concatenate([lanes(z[i : i + K], index[i : i + K]) for i in (0, K)], axis=0)
             out = jnp.where(block == b, g, out)
         gt[where, :] = out
@@ -250,7 +276,7 @@
     for dx in (0, 1, 3, 2):
         pick(dx, core)
     arrived(0, m0)
-    got = m0[:, 0, :].T
+    got = m0[...].T
     asked = got[K * B : K * B + K].astype(I32)
     onehot = jnp.concatenate(
         [jnp.where(sub == asked[r : r + 1, :], 1.0, 0.0).astype(BF16) for r in range(K)], axis=1
@@ -262,40 +288,39 @@
     q0 = partial + forward(gt[...].T)
 
     w0 = blocks_times(p_v, q0)
-    c0_part = jnp.sum(z0 * q0)
+    even, odd = pl.ds(0, N, stride=2), pl.ds(1, N, stride=2)
+    s2[odd, :] = answers(w0, asked)
+    c0_part = total(z0 * q0)
     out = to_owners(spread(w0))
-    s2[:, 0, :] = jnp.where(lane == 80, rho0_part, jnp.where(lane == 81, c0_part, out))
-    s2[:, 1, :] = answers(w0, asked)
-    exchange(2, s2, m2)
+    s2[even, :] = jnp.where(lane == 80, rho0_part, jnp.where(lane == 81, c0_part, out))
+    exchange(2, s2, m2, rows=2)
     partial = blocks_times(d_v, w0)
-    arrived(2, m2)
-    first = m2[:, 0, :]
+    arrived(2, m2, rows=2)
+    first = m2[even, :]
     sums = jnp.sum(first, axis=0, keepdims=True)
     lane1 = iota((1, N), 1)
-    rho0 = jnp.sum(jnp.where(lane1 == 80, sums, 0.0))
-    c0 = jnp.sum(jnp.where(lane1 == 81, sums, 0.0))
-    alpha = jnp.full((1, 1), rho0, F32) / jnp.full((1, 1), c0, F32)
-    image = partial + scatter(first.T, onehot) + forward(m2[:, 1, :].T)
+    rho0, c0 = (total(jnp.where(lane1 == i, sums, 0.0)) for i in (80, 81))
+    alpha = rho0 / c0
+    image = partial + forward(m2[odd, :].T) + scatter(first.T, onehot)
 
     r1 = rhs - alpha * q0
     z1 = z0 - alpha * w0
     y1 = q0 - alpha * image
-    rho1_part, c1_part, e1_part = jnp.sum(r1 * z1), jnp.sum(z1 * y1), jnp.sum(z1 * q0)
-    s3[0] = jnp.where(
+    rho1_part, c1_part, e1_part = total(r1 * z1), total(z1 * y1), total(z1 * q0)
+    s3[...] = jnp.where(
         lane1 == 0, rho1_part, jnp.where(lane1 == 1, c1_part, jnp.where(lane1 == 2, e1_part, 0.0))
     )
     exchange(3, s3, m3, one=True)
     arrived(3, m3)
-    sums = jnp.sum(m3[:, 0, :], axis=0, keepdims=True)
-    rho1, c1, e1 = (
-        jnp.full((1, 1), jnp.sum(jnp.where(lane1 == i, sums, 0.0)), F32) for i in range(3)
-    )
-    beta = rho1 / jnp.full((1, 1), rho0, F32)
-    step = rho1 / (c1 + 2.0 * beta * e1 + beta * beta * jnp.full((1, 1), c0, F32))
+    sums = jnp.sum(m3[...], axis=0, keepdims=True)
+    rho1, c1, e1 = (total(jnp.where(lane1 == i, sums, 0.0)) for i in range(3))
+    beta = rho1 / rho0
+    step = rho1 / (c1 + 2.0 * beta * e1 + beta * beta * c0)
     o_ref[0] = alpha * z0 + step * (z1 + beta * z0)
     o_ref[1] = r1 - step * (y1 + beta * q0)
-    for n, src in ((0, m0), (2, m2), (3, m3)):
-        pltpu.make_async_copy(src.at[0 : N - 1], src.at[0 : N - 1], send.at[n]).wait()
+    for n, dst, rows in ((0, m0, 1), (2, m2, 2), (3, m3, 1)):
+        most = dst.at[0 : rows * (N - 1)]
+        pltpu.make_async_copy(most, most, send.at[n]).wait()
     pltpu.make_async_copy(
         tiles.at[:, 0 : CHIPS - 1], tiles.at[:, 0 : CHIPS - 1], send.at[1]
     ).wait()
@@ -307,7 +332,7 @@
     shape = jax.ShapeDtypeStruct((B, N), F32)
     any_space = pl.BlockSpec(memory_space=pltpu.HBM)
     vmem = pl.BlockSpec(memory_space=pltpu.VMEM)
-    row, two = pltpu.VMEM((N, 1, N), F32), pltpu.VMEM((N, 2, N), F32)
+    row, two = pltpu.VMEM((N, N), F32), pltpu.VMEM((2 * N, N), F32)
     out = pl.pallas_call(
         kernel,
         out_shape=jax.ShapeDtypeStruct((2, B, N), F32),
@@ -321,10 +346,10 @@
             pltpu.VMEM((K, N), I32),
             pltpu.VMEM((N, N), I32),
             pltpu.SemaphoreType.DMA((6,)),
-            row, row, pltpu.VMEM((B, 1, N), F32), pltpu.VMEM((B, N, 1, N), F32),
-            two, two, pltpu.VMEM((1, 1, N), F32), row,
+            row, row, pltpu.VMEM((B, N), F32), pltpu.VMEM((B, N, N), F32),
+            two, two, pltpu.VMEM((1, N), F32), row,
             *[pltpu.SemaphoreType.DMA((4,))] * 5,
-            pltpu.VMEM((K * B, N), F32),
+            pltpu.VMEM((N, N), F32),
             pltpu.VMEM((K * B, N), F32),
             pltpu.VMEM((N, N), I32),
             pltpu.VMEM((N, N), F32),

time: 34.1 us -> 33.2 us (0.974)
  Pallas kernels: 32.7 us -> 31.8 us
    pallas_call x1, Pallas kernels: 32.7 us -> 31.8 us  [solve(): pl.pallas_call(kernel, out_shape=jax.ShapeDtypeStruct((2, B, N), F32), in...]
where the time goes in v4:
time: 33.2 us; the launch traced here: 33.1 us
  Pallas kernels  31.8 us (96%)
  between operations  0.64 us (2%)
  local copies, waits for them, and re-layouts  0.61 us (2%)
    pallas_call x1, Pallas kernels, solve(): pl.pallas_call(kernel, out_shape=jax.ShapeDtypeStruct((2, B, N), F32), in...  31.8 us

profile of v4, /device:TPU:1, one launch (start us, length us, event | category | flops | bytes accessed | tf_op | source)
XLA Modules:
  0.0 33.1 jit_solution(11439129938381698816)
XLA Ops:
  0.6 31.8 %shard_map.77 = f32[2,9,128]{2,1,0:T(8,128)S(1)} custom-call(f32[9,128]{1,0:T(8,128)} %b_hbm.1, f32[9,9,128]{2,1,0:T(8,128)} %d_hbm.1, f32[9,9,128]{2,1,0:T(8,128)} %p_hbm.1, f32[9,9,8,128]{3,2,1,0:T(8,128)} %bitcast.6, s32[8,128]{1,0:T(8,128)} %c_hbm.1, s32[128,128]{1,0:T(8,128)} %bitcast.7), custom_call_target="tpu_custom_call" | custom-call | tf_op jit(solution)/shard_map/pallas_call | solution.py:336
  32.5 0.6 %slice_bitcast_fusion = (f32[9,128]{1,0:T(8,128)}, f32[9,128]{1,0:T(8,128)}) fusion(f32[2,9,128]{2,1,0:T(8,128)S(1)} %shard_map.77), kind=kLoop, calls=%fused_computation | loop fusion | bytes 18432 | tf_op jit(solution)/shard_map/squeeze | solution.py:371

commit v5 on v4

--- a/solution.py
+++ b/solution.py
@@ -174,20 +174,25 @@
             out.append(total)
         return out
 
+    which = jnp.concatenate(
+        [
+            jnp.concatenate([jnp.where(p, float(k), 0.0) for k, p in enumerate(places)], axis=1),
+            jnp.concatenate([jnp.where(p, iota((K, N), 1), 0).astype(F32) for p in places], axis=1),
+        ],
+        axis=0,
+    )
+    which = dot_t(which.astype(BF16), by_owner).astype(I32)
+    list_at, slot_at = which[0:K], which[K : 2 * K]
+
+    def bucket(e):
+        out = lanes(rows8(e[0:1, :]), slot_at)
+        for k in range(1, K):
+            out = jnp.where(list_at == k, lanes(rows8(e[k : k + 1, :]), slot_at), out)
+        return out
+
     def to_owners(lists):
-        wide = jnp.concatenate(
-            [
-                jnp.concatenate(
-                    [jnp.where(places[k], rows8(e[k : k + 1, :]), 0.0) for k in range(K)], axis=1
-                )
-                for e in lists
-            ]
-            + [jnp.zeros((N - K * len(lists), K * N), F32)],
-            axis=0,
-        )
-        h, m, l = pieces(wide)
-        both = dot_t(by_owner, jnp.concatenate([h, m], axis=0))
-        return both[:, 0:N] + both[:, N:] + dot_t(by_owner, l)
+        rest = jnp.zeros((N - K * len(lists), N), F32)
+        return jnp.concatenate(lists + [rest] if rest.shape[0] else lists, axis=0).T
 
     def answers(v, asked):
         parts = [lanes(rows8(v[b : b + 1]), asked) for b in range(B)]
@@ -218,12 +223,9 @@
     tile[...] = z0
     copies[4].wait()
     copies[5].wait()
-    s0[...] = to_owners(spread(z0) + [offset.astype(F32)])
-    wanted = jnp.concatenate(
-        [jnp.where(places[k], rows8(offset[k : k + 1, :]), 0).astype(F32) for k in range(K)], axis=1
-    )
-    wanted = jnp.concatenate([wanted] * (N // K), axis=0).astype(BF16)
-    wanted = dot_t(by_owner, wanted).astype(I32)
+    bucket_offset = bucket(offset.astype(F32))
+    s0[...] = to_owners([bucket(e) for e in spread(z0)] + [bucket_offset])
+    wanted = to_owners([bucket_offset] * (N // K)).astype(I32)
     pl.semaphore_wait(barrier, N - 1)
 
     for dx in (2, 1, 3, 0):
@@ -291,7 +293,7 @@
     even, odd = pl.ds(0, N, stride=2), pl.ds(1, N, stride=2)
     s2[odd, :] = answers(w0, asked)
     c0_part = total(z0 * q0)
-    out = to_owners(spread(w0))
+    out = to_owners([bucket(e) for e in spread(w0)])
     s2[even, :] = jnp.where(lane == 80, rho0_part, jnp.where(lane == 81, c0_part, out))
     exchange(2, s2, m2, rows=2)
     partial = blocks_times(d_v, w0)

time: 33.2 us -> 33 us (level)
  no operation moved by 1% of the time
where the time goes in v5:
time: 33 us; the launch traced here: 32.8 us
  Pallas kernels  31.6 us (96%)
  between operations  0.64 us (2%)
  local copies, waits for them, and re-layouts  0.61 us (2%)
    pallas_call x1, Pallas kernels, solve(): pl.pallas_call(kernel, out_shape=jax.ShapeDtypeStruct((2, B, N), F32), in...  31.6 us

profile of v5, /device:TPU:1, one launch (start us, length us, event | category | flops | bytes accessed | tf_op | source)
XLA Modules:
  0.0 32.8 jit_solution(16807476892179754198)
XLA Ops:
  0.6 31.6 %shard_map.77 = f32[2,9,128]{2,1,0:T(8,128)S(1)} custom-call(f32[9,128]{1,0:T(8,128)} %b_hbm.1, f32[9,9,128]{2,1,0:T(8,128)} %d_hbm.1, f32[9,9,128]{2,1,0:T(8,128)} %p_hbm.1, f32[9,9,8,128]{3,2,1,0:T(8,128)} %bitcast.6, s32[8,128]{1,0:T(8,128)} %c_hbm.1, s32[128,128]{1,0:T(8,128)} %bitcast.7), custom_call_target="tpu_custom_call" | custom-call | tf_op jit(solution)/shard_map/pallas_call | solution.py:338
  32.2 0.6 %slice_bitcast_fusion = (f32[9,128]{1,0:T(8,128)}, f32[9,128]{1,0:T(8,128)}) fusion(f32[2,9,128]{2,1,0:T(8,128)S(1)} %shard_map.77), kind=kLoop, calls=%fused_computation | loop fusion | bytes 18432 | tf_op jit(solution)/shard_map/squeeze | solution.py:373

commit v6 on v5

--- a/solution.py
+++ b/solution.py
@@ -87,7 +87,7 @@
 def kernel(
     b_hbm, d_hbm, p_hbm, u_hbm, c_hbm, t_hbm, o_ref,
     b_v, d_v, p_v, u_v, c_v, t_v, in_sem,
-    s0, m0, tile, tiles, s2, m2, s3, m3, send, recv, plane_recv, half_send, half_recv, pt, ft, wt, gt,
+    s0, m0, tile, tiles, s2, m2, s3, m3, send, recv, plane_recv, half_send, half_recv, pt, ft, wt, gt, wt2, po, tell_sem,
 ):
     me = lax.axis_index("rows")
     mine = place_of(me)
@@ -133,9 +133,8 @@
         most = dst.at[0 : rows * (N - 1)]
         pltpu.make_async_copy(most, most, recv.at[n]).wait()
 
-    def plane(dx, half):
-        x = lax.rem(me // 32 - dx + 4, 4)
-        return pl.ds(pl.multiple_of(half * CHIPS + x * PLANE, PLANE), PLANE)
+    def plane(dx):
+        return pl.multiple_of(lax.rem(me // 32 - dx + 4, 4) * PLANE, PLANE)
 
     copies[0].wait()
     copies[1].wait()
@@ -226,7 +225,18 @@
     bucket_offset = bucket(offset.astype(F32))
     s0[...] = to_owners([bucket(e) for e in spread(z0)] + [bucket_offset])
     wanted = to_owners([bucket_offset] * (N // K)).astype(I32)
+    wt[...] = wanted
     pl.semaphore_wait(barrier, N - 1)
+
+    tell = pltpu.make_async_remote_copy(
+        src_ref=wt.at[pl.ds((1 - core) * CHIPS, CHIPS)],
+        dst_ref=wt2,
+        send_sem=tell_sem.at[0],
+        recv_sem=tell_sem.at[1],
+        device_id=(peers.device((0, 0, 0, 1)),),
+        device_id_type=MESH,
+    )
+    tell.start()
 
     for dx in (2, 1, 3, 0):
         for d in STEPS:
@@ -245,15 +255,28 @@
     lane = iota((N, N), 1)
     partial = blocks_times(d_v, z0)
     rho0_part = total(rhs * z0)
+    block = iota((PLANE, N), 1) >> 3
+
+    def pick(chips, index):
+        here = pl.ds(core * CHIPS + chips, PLANE)
+        out = jnp.zeros((PLANE, N), F32)
+        for b in range(B):
+            z = tiles[b, here, :]
+            g = jnp.concatenate([lanes(z[i : i + K], index[i : i + K]) for i in (0, K)], axis=0)
+            out = jnp.where(block == b, g, out)
+        return out
+
+    tell.wait_recv()
     halves = []
     for dx in (0, 1, 3, 2):
         n = PLANE - (dx == 0)
         pltpu.make_async_copy(tiles.at[:, 0:n], tiles.at[:, 0:n], plane_recv.at[dx]).wait()
-        here = tiles.at[:, plane(dx, core)]
+        there = pl.ds(plane(dx), PLANE)
+        po[there, :] = pick(plane(dx), wt2[there, :])
         halves.append(
             pltpu.make_async_remote_copy(
-                src_ref=here,
-                dst_ref=here,
+                src_ref=po.at[there],
+                dst_ref=gt.at[pl.ds(core * CHIPS + plane(dx), PLANE)],
                 send_sem=half_send.at[dx],
                 recv_sem=half_recv.at[dx],
                 device_id=(peers.device((0, 0, 0, 1)),),
@@ -261,22 +284,9 @@
             )
         )
         halves[-1].start()
-
-    block = iota((PLANE, N), 1) >> 3
-    wt[...] = wanted
-
-    def pick(dx, half):
-        where = plane(dx, half)
-        index = wt[where, :]
-        out = jnp.zeros((PLANE, N), F32)
-        for b in range(B):
-            z = tiles[b, where, :]
-            g = jnp.concatenate([lanes(z[i : i + K], index[i : i + K]) for i in (0, K)], axis=0)
-            out = jnp.where(block == b, g, out)
-        gt[where, :] = out
-
     for dx in (0, 1, 3, 2):
-        pick(dx, core)
+        here = pl.ds(core * CHIPS + plane(dx), PLANE)
+        gt[here, :] = pick(plane(dx), wt[here, :])
     arrived(0, m0)
     got = m0[...].T
     asked = got[K * B : K * B + K].astype(I32)
@@ -284,9 +294,8 @@
         [jnp.where(sub == asked[r : r + 1, :], 1.0, 0.0).astype(BF16) for r in range(K)], axis=1
     )
     partial = partial + scatter(got, onehot)
-    for n, dx in enumerate((0, 1, 3, 2)):
-        halves[n].wait_recv()
-        pick(dx, 1 - core)
+    for h in halves:
+        h.wait_recv()
     q0 = partial + forward(gt[...].T)
 
     w0 = blocks_times(p_v, q0)
@@ -326,7 +335,7 @@
     pltpu.make_async_copy(
         tiles.at[:, 0 : CHIPS - 1], tiles.at[:, 0 : CHIPS - 1], send.at[1]
     ).wait()
-    for h in halves:
+    for h in [tell] + halves:
         h.wait_send()
 
 
@@ -355,6 +364,9 @@
             pltpu.VMEM((K * B, N), F32),
             pltpu.VMEM((N, N), I32),
             pltpu.VMEM((N, N), F32),
+            pltpu.VMEM((CHIPS, N), I32),
+            pltpu.VMEM((CHIPS, N), F32),
+            pltpu.SemaphoreType.DMA((2,)),
         ],
         compiler_params=pltpu.CompilerParams(collective_id=0, has_side_effects=True, vmem_limit_bytes=8 << 20),
     )(

time: 33 us -> 32.8 us (level)
  no operation moved by 1% of the time
where the time goes in v6:
time: 32.8 us; the launch traced here: 32.7 us
  Pallas kernels  31.5 us (96%)
  between operations  0.64 us (2%)
  local copies, waits for them, and re-layouts  0.61 us (2%)
    pallas_call x1, Pallas kernels, solve(): pl.pallas_call(kernel, out_shape=jax.ShapeDtypeStruct((2, B, N), F32), in...  31.5 us

profile of v6, /device:TPU:1, one launch (start us, length us, event | category | flops | bytes accessed | tf_op | source)
XLA Modules:
  0.0 32.7 jit_solution(17885407942287401643)
XLA Ops:
  0.6 31.5 %shard_map.77 = f32[2,9,128]{2,1,0:T(8,128)S(1)} custom-call(f32[9,128]{1,0:T(8,128)} %b_hbm.1, f32[9,9,128]{2,1,0:T(8,128)} %d_hbm.1, f32[9,9,128]{2,1,0:T(8,128)} %p_hbm.1, f32[9,9,8,128]{3,2,1,0:T(8,128)} %bitcast.6, s32[8,128]{1,0:T(8,128)} %c_hbm.1, s32[128,128]{1,0:T(8,128)} %bitcast.7), custom_call_target="tpu_custom_call" | custom-call | tf_op jit(solution)/shard_map/pallas_call | solution.py:347
  32.1 0.6 %slice_bitcast_fusion = (f32[9,128]{1,0:T(8,128)}, f32[9,128]{1,0:T(8,128)}) fusion(f32[2,9,128]{2,1,0:T(8,128)S(1)} %shard_map.77), kind=kLoop, calls=%fused_computation | loop fusion | bytes 18432 | tf_op jit(solution)/shard_map/squeeze | solution.py:385

commit v7 on v6

--- a/solution.py
+++ b/solution.py
@@ -29,9 +29,9 @@
 
 class Peers:
     def __init__(self, me):
-        x, y, z, c = me // 32, lax.rem(me // 8, 4), lax.rem(me // 2, 4), lax.rem(me, 2)
-        self.x = [lax.rem(x + d, 4) * 16 for d in range(4)]
-        self.yz = [[lax.rem(y + i, 4) * 4 + lax.rem(z + j, 4) for j in range(4)] for i in range(4)]
+        x, y, z, c = me >> 5, (me >> 3) & 3, (me >> 1) & 3, me & 1
+        self.x = [((x + d) & 3) * 16 for d in range(4)]
+        self.yz = [[((y + i) & 3) * 4 + ((z + j) & 3) for j in range(4)] for i in range(4)]
         self.core = [c, 1 - c]
         self.half = [c * CHIPS, CHIPS - c * CHIPS]
 
@@ -322,6 +322,14 @@
         lane1 == 0, rho1_part, jnp.where(lane1 == 1, c1_part, jnp.where(lane1 == 2, e1_part, 0.0))
     )
     exchange(3, s3, m3, one=True)
+    for n, dst, rows in ((0, m0, 1), (2, m2, 2)):
+        most = dst.at[0 : rows * (N - 1)]
+        pltpu.make_async_copy(most, most, send.at[n]).wait()
+    pltpu.make_async_copy(
+        tiles.at[:, 0 : CHIPS - 1], tiles.at[:, 0 : CHIPS - 1], send.at[1]
+    ).wait()
+    for h in [tell] + halves:
+        h.wait_send()
     arrived(3, m3)
     sums = jnp.sum(m3[...], axis=0, keepdims=True)
     rho1, c1, e1 = (total(jnp.where(lane1 == i, sums, 0.0)) for i in range(3))
@@ -329,14 +337,8 @@
     step = rho1 / (c1 + 2.0 * beta * e1 + beta * beta * c0)
     o_ref[0] = alpha * z0 + step * (z1 + beta * z0)
     o_ref[1] = r1 - step * (y1 + beta * q0)
-    for n, dst, rows in ((0, m0, 1), (2, m2, 2), (3, m3, 1)):
-        most = dst.at[0 : rows * (N - 1)]
-        pltpu.make_async_copy(most, most, send.at[n]).wait()
-    pltpu.make_async_copy(
-        tiles.at[:, 0 : CHIPS - 1], tiles.at[:, 0 : CHIPS - 1], send.at[1]
-    ).wait()
-    for h in [tell] + halves:
-        h.wait_send()
+    most = m3.at[0 : N - 1]
+    pltpu.make_async_copy(most, most, send.at[3]).wait()
 
 
 def solve(right_side, diag_blocks, precond, upper_blocks, block_cols, slot_of_camera):

time: 32.8 us -> 32.8 us (level)
  no operation moved by 1% of the time
where the time goes in v7:
time: 32.8 us; the launch traced here: 32.7 us
  Pallas kernels  31.4 us (96%)
  between operations  0.64 us (2%)
  local copies, waits for them, and re-layouts  0.61 us (2%)
    pallas_call x1, Pallas kernels, solve(): pl.pallas_call(kernel, out_shape=jax.ShapeDtypeStruct((2, B, N), F32), in...  31.4 us

profile of v7, /device:TPU:1, one launch (start us, length us, event | category | flops | bytes accessed | tf_op | source)
XLA Modules:
  0.0 32.7 jit_solution(4152830487371084271)
XLA Ops:
  0.6 31.4 %shard_map.77 = f32[2,9,128]{2,1,0:T(8,128)S(1)} custom-call(f32[9,128]{1,0:T(8,128)} %b_hbm.1, f32[9,9,128]{2,1,0:T(8,128)} %d_hbm.1, f32[9,9,128]{2,1,0:T(8,128)} %p_hbm.1, f32[9,9,8,128]{3,2,1,0:T(8,128)} %bitcast.6, s32[8,128]{1,0:T(8,128)} %c_hbm.1, s32[128,128]{1,0:T(8,128)} %bitcast.7), custom_call_target="tpu_custom_call" | custom-call | tf_op jit(solution)/shard_map/pallas_call | solution.py:349
  32.1 0.6 %slice_bitcast_fusion = (f32[9,128]{1,0:T(8,128)}, f32[9,128]{1,0:T(8,128)}) fusion(f32[2,9,128]{2,1,0:T(8,128)S(1)} %shard_map.77), kind=kLoop, calls=%fused_computation | loop fusion | bytes 18432 | tf_op jit(solution)/shard_map/squeeze | solution.py:387

commit v8 on v6

--- a/solution.py
+++ b/solution.py
@@ -220,24 +220,7 @@
     rhs = b_v[...]
     z0 = blocks_times(p_v, rhs)
     tile[...] = z0
-    copies[4].wait()
-    copies[5].wait()
-    bucket_offset = bucket(offset.astype(F32))
-    s0[...] = to_owners([bucket(e) for e in spread(z0)] + [bucket_offset])
-    wanted = to_owners([bucket_offset] * (N // K)).astype(I32)
-    wt[...] = wanted
     pl.semaphore_wait(barrier, N - 1)
-
-    tell = pltpu.make_async_remote_copy(
-        src_ref=wt.at[pl.ds((1 - core) * CHIPS, CHIPS)],
-        dst_ref=wt2,
-        send_sem=tell_sem.at[0],
-        recv_sem=tell_sem.at[1],
-        device_id=(peers.device((0, 0, 0, 1)),),
-        device_id_type=MESH,
-    )
-    tell.start()
-
     for dx in (2, 1, 3, 0):
         for d in STEPS:
             if d[0] == dx and d[3] == 0:
@@ -249,6 +232,23 @@
                     device_id=(peers.device(d),),
                     device_id_type=MESH,
                 ).start()
+    copies[4].wait()
+    copies[5].wait()
+    bucket_offset = bucket(offset.astype(F32))
+    s0[...] = to_owners([bucket(e) for e in spread(z0)] + [bucket_offset])
+    wanted = to_owners([bucket_offset] * (N // K)).astype(I32)
+    wt[...] = wanted
+
+    tell = pltpu.make_async_remote_copy(
+        src_ref=wt.at[pl.ds((1 - core) * CHIPS, CHIPS)],
+        dst_ref=wt2,
+        send_sem=tell_sem.at[0],
+        recv_sem=tell_sem.at[1],
+        device_id=(peers.device((0, 0, 0, 1)),),
+        device_id_type=MESH,
+    )
+    tell.start()
+
     exchange(0, s0, m0)
     tiles[:, mine] = tile[...]
 

time: 32.8 us -> 32.8 us (level)
  no operation moved by 1% of the time
where the time goes in v8:
time: 32.8 us; the launch traced here: 32.7 us
  Pallas kernels  31.4 us (96%)
  between operations  0.64 us (2%)
  local copies, waits for them, and re-layouts  0.61 us (2%)
    pallas_call x1, Pallas kernels, solve(): pl.pallas_call(kernel, out_shape=jax.ShapeDtypeStruct((2, B, N), F32), in...  31.4 us

profile of v8, /device:TPU:1, one launch (start us, length us, event | category | flops | bytes accessed | tf_op | source)
XLA Modules:
  0.0 32.7 jit_solution(4853586871741179812)
XLA Ops:
  0.6 31.4 %shard_map.77 = f32[2,9,128]{2,1,0:T(8,128)S(1)} custom-call(f32[9,128]{1,0:T(8,128)} %b_hbm.1, f32[9,9,128]{2,1,0:T(8,128)} %d_hbm.1, f32[9,9,128]{2,1,0:T(8,128)} %p_hbm.1, f32[9,9,8,128]{3,2,1,0:T(8,128)} %bitcast.6, s32[8,128]{1,0:T(8,128)} %c_hbm.1, s32[128,128]{1,0:T(8,128)} %bitcast.7), custom_call_target="tpu_custom_call" | custom-call | tf_op jit(solution)/shard_map/pallas_call | solution.py:347
  32.1 0.6 %slice_bitcast_fusion = (f32[9,128]{1,0:T(8,128)}, f32[9,128]{1,0:T(8,128)}) fusion(f32[2,9,128]{2,1,0:T(8,128)S(1)} %shard_map.77), kind=kLoop, calls=%fused_computation | loop fusion | bytes 18432 | tf_op jit(solution)/shard_map/squeeze | solution.py:385
